TPU v7x, 32 devices: a whole 2x2x4 slice. The times are simulated.
32 devices in a mesh: row: 4 (over y, core), col: 8 (over z, x).
Axes of the slice: x: 2, y: 2, z: 4, core: 2. Of those that a mesh axis runs over, the one named last changes fastest.
Arguments:
- positions: float32 [3, 512], P(None, ('row', 'col')), as said below
- thermal_noise: float32 [32, 3, 512], P(None, None, ('row', 'col')), as said below
Outputs:
- displacement: float32 [32, 3, 512], P(None, None, ('row', 'col'))
Inputs may be any that keep to these rules, and one draw needn't show every extreme that they name: `positions`: any two particles are at least 1.0 apart. `thermal_noise`: finite real entries.
All inputs are finite; a program needn't handle non-finite values.
Results may differ from a plain program's by a relative error of at most 0.0013.
Values may be sent and summed in bfloat16 or wider, within the bound.
A program may use at most 64 MiB of HBM per device.

v0:
```python
import jax
import jax.numpy as jnp
from jax import lax
from jax.sharding import PartitionSpec as P


def pair_tensor(rows_pos, cols_pos, retain):
    offsets = [rows_pos[a][None, :] - cols_pos[a][:, None] for a in range(3)]
    squared = offsets[0] * offsets[0] + offsets[1] * offsets[1] + offsets[2] * offsets[2]
    guarded = jnp.where(retain, squared, 4.0)
    inverse = lax.rsqrt(guarded)
    distance = guarded * inverse
    correlation = distance < 2.0
    inverse_cube = inverse * inverse * inverse
    inverse_fifth = inverse_cube * inverse * inverse
    isotropic = jnp.where(
        correlation, 1.0 - 0.28125 * distance, 0.75 * inverse + 0.5 * inverse_cube
    )
    dyadic = jnp.where(correlation, 0.09375 * inverse, 0.75 * inverse_cube - 1.5 * inverse_fifth)
    isotropic = jnp.where(retain, isotropic, 0.0)
    dyadic = jnp.where(retain, dyadic, 0.0)
    columns = []
    for b in range(3):
        elements = []
        for a in range(3):
            element = dyadic * offsets[a] * offsets[b]
            if a == b:
                element = element + isotropic
            elements.append(element)
        columns.append(jnp.stack(elements, axis=1))
    return jnp.stack(columns, axis=0)


def half_image(pos_rows, pos_cols, vec_rows, vec_cols, own_vector):
    row_devices = lax.axis_size("row")
    col_devices = lax.axis_size("col")
    row_index = lax.axis_index("row")
    col_index = lax.axis_index("col")
    samples = own_vector.shape[0]
    per_device = own_vector.shape[2]
    row_count = pos_rows.shape[1]
    row_label = row_index * col_devices * per_device + lax.iota(jnp.int32, row_count)
    group_size = min(row_devices, max(1, 128 // per_device))
    width = group_size * per_device
    group_count = row_devices // group_size
    sum_rows = jnp.zeros((samples, 3, row_count), jnp.float32)
    sum_cols = jnp.zeros((samples, 3, per_device * row_devices), jnp.float32)

    def add_group(group, totals):
        sum_rows, sum_cols = totals
        start = group * width
        cols_pos = lax.dynamic_slice_in_dim(pos_cols, start, width, 1)
        cols_vec = lax.dynamic_slice_in_dim(vec_cols, start, width, 2)
        local_cols = lax.iota(jnp.int32, width)
        segment = group * group_size + local_cols // per_device
        col_label = (segment * col_devices + col_index) * per_device + local_cols % per_device
        keep = segment >= row_index
        upper = (segment != row_index)[:, None] | (row_label[None, :] < col_label[:, None])
        retain = keep[:, None] & upper & (row_label[None, :] != col_label[:, None])
        tensor = pair_tensor(pos_rows, cols_pos, retain).astype(jnp.bfloat16)
        sum_rows = sum_rows + jnp.einsum(
            "kbj,bjai->kai", cols_vec, tensor, preferred_element_type=jnp.float32
        )
        credit = jnp.einsum("kai,bjai->kbj", vec_rows, tensor, preferred_element_type=jnp.float32)
        previous = lax.dynamic_slice_in_dim(sum_cols, start, width, 2)
        sum_cols = lax.dynamic_update_slice_in_dim(sum_cols, previous + credit, start, 2)
        return (sum_rows, sum_cols)

    totals = (sum_rows, sum_cols)
    totals = lax.fori_loop(row_index // group_size, group_count, add_group, totals)
    sum_rows, sum_cols = totals
    mobility_image = own_vector + lax.psum_scatter(sum_rows, "col", scatter_dimension=2, tiled=True)
    return mobility_image + lax.psum_scatter(sum_cols, "row", scatter_dimension=2, tiled=True)


def on_device(positions, thermal_noise):
    squares = lax.psum(jnp.sum(thermal_noise * thermal_noise, axis=(1, 2)), ("row", "col"))
    noise_length = jnp.sqrt(squares + 1e-06)
    basis_one = thermal_noise / noise_length[:, None, None]
    pos_cols, cols_one = (
        lax.all_gather(positions, "row", axis=1, tiled=True),
        lax.all_gather(basis_one, "row", axis=2, tiled=True),
    )
    pos_rows, rows_wide = (
        lax.all_gather(positions, "col", axis=1, tiled=True),
        lax.all_gather(basis_one, "col", axis=2, tiled=True),
    )
    image_one = half_image(
        pos_rows, pos_cols, rows_wide.astype(jnp.bfloat16), cols_one.astype(jnp.bfloat16), basis_one
    )
    alpha_one = lax.psum(jnp.sum(basis_one * image_one, axis=(1, 2)), ("row", "col"))
    remainder = image_one - alpha_one[:, None, None] * basis_one
    beta_squared = lax.psum(jnp.sum(remainder * remainder, axis=(1, 2)), ("row", "col"))
    beta_one = jnp.sqrt(beta_squared + 1e-06)
    basis_two = remainder / beta_one[:, None, None]
    narrow_two = basis_two.astype(jnp.bfloat16)
    cols_two = lax.all_gather(narrow_two, "row", axis=2, tiled=True)
    rows_two = lax.all_gather(narrow_two, "col", axis=2, tiled=True)
    image_two = half_image(pos_rows, pos_cols, rows_two, cols_two, basis_two)
    alpha_two = lax.psum(jnp.sum(basis_two * image_two, axis=(1, 2)), ("row", "col"))
    det_root = jnp.sqrt(alpha_one * alpha_two - beta_one * beta_one)
    trace_root = jnp.sqrt(alpha_one + alpha_two + 2.0 * det_root)
    weight_one = (alpha_one + det_root) / trace_root
    weight_two = beta_one / trace_root
    return (
        0.5
        * noise_length[:, None, None]
        * (weight_one[:, None, None] * basis_one + weight_two[:, None, None] * basis_two)
    )


def solution(mesh):
    return jax.shard_map(
        on_device,
        mesh=mesh,
        in_specs=(P(None, ("row", "col")), P(None, None, ("row", "col"))),
        out_specs=P(None, None, ("row", "col")),
        check_vma=False,
    )
```

profile of v0, /device:TPU:0, one launch (start us, length us, event | category | flops | bytes accessed | tf_op | source)
XLA Modules:
  0.0 451.7 jit_solution(3374881495807771110)
XLA Ops:
  6.5 0.7 copy-done.3
  7.2 28.1 %all-gather = f32[8,16,3]{1,2,0:T(4,128)S(1)} all-gather(f32[1,16,3]{1,2,0:T(4,128)S(1)} %bitcast.133), channel_id=1, replica_groups=mesh['row'=4,'col'=8] {'col'}, dimensions={0}, use_global_device_ids=true | all-gather | bytes 1728 | tf_op jit(solution)/shard_map/all_gather | solution.py:85
  35.3 5.2 %all-gather.1 = f32[4,16,3]{1,2,0:T(4,128)S(1)} all-gather(f32[1,16,3]{1,2,0:T(4,128)S(1)} %bitcast.134), channel_id=1, replica_groups=mesh['row'=4,'col'=8] {'row'}, dimensions={0}, use_global_device_ids=true | all-gather | bytes 960 | tf_op jit(solution)/shard_map/all_gather | solution.py:81
  40.5 38.9 %psum.28 = f32[32]{0:T(128)S(1)} all-reduce(f32[32]{0:T(128)S(1)} %multiply_reduce_fusion.3), channel_id=1, replica_groups=mesh['row'=4,'col'=8] {'row','col'}, use_global_device_ids=true, to_apply=%region_1.0 | all-reduce | flops 32 | bytes 256 | tf_op jit(solution)/shard_map/psum | solution.py:77
  79.5 5.5 %all_gather.20 = bf16[32,3,64]{0,2,1:T(8,128)(2,1)S(1)} all-gather(bf16[32,3,16]{0,2,1:T(8,128)(2,1)S(1)} %convert.110), channel_id=1, replica_groups=mesh['row'=4,'col'=8] {'row'}, dimensions={2}, use_global_device_ids=true | all-gather | bytes 15360 | tf_op jit(solution)/shard_map/all_gather | solution.py:82
  85.1 30.6 %all_gather.21 = bf16[32,3,128]{0,2,1:T(8,128)(2,1)S(1)} all-gather(bf16[32,3,16]{0,2,1:T(8,128)(2,1)S(1)} %get-tuple-element.415), channel_id=1, replica_groups=mesh['row'=4,'col'=8] {'col'}, dimensions={2}, use_global_device_ids=true | all-gather | bytes 27648 | tf_op jit(solution)/shard_map/all_gather | solution.py:86
  115.9 0.7 while.30
  116.6 0.7 copy.42
  117.5 0.8 copy.41
  118.3 17.6 %reduce-scatter.7.cloned.1.call-done = f32[32,3,16]{0,2,1:T(8,128)} async-done(((f32[32,3,64]{0,2,1:T(8,128)}), f32[32,3,16]{0,2,1:T(8,128)}) %reduce-scatter.7.cloned.1.call-update) | async-done | bytes 6160 | tf_op jit(solution)/shard_map/reduce_scatter | solution.py:73
  135.9 65.3 %reduce-scatter.5.cloned.1.call-done = f32[32,3,16]{0,2,1:T(8,128)} async-done(((f32[32,3,128]{0,2,1:T(8,128)}), f32[32,3,16]{0,2,1:T(8,128)}) %reduce-scatter.5.cloned.1.call-update) | async-done | bytes 6160 | tf_op jit(solution)/shard_map/reduce_scatter | solution.py:72
  201.2 0.8 multiply_reduce_fusion.2
  202.1 40.1 %psum.29 = f32[32]{0:T(128)S(1)} all-reduce(f32[32]{0:T(128)S(1)} %multiply_reduce_fusion.2), channel_id=1, replica_groups=mesh['row'=4,'col'=8] {'row','col'}, use_global_device_ids=true, to_apply=%region_7.8 | all-reduce | flops 32 | bytes 256 | tf_op jit(solution)/shard_map/psum | solution.py:91
  242.2 39.1 %psum.30 = f32[32]{0:T(128)S(1)} all-reduce(f32[32]{0:T(128)S(1)} %get-tuple-element.413), channel_id=1, replica_groups=mesh['row'=4,'col'=8] {'row','col'}, use_global_device_ids=true, to_apply=%region_9.10 | all-reduce | flops 32 | bytes 256 | tf_op jit(solution)/shard_map/psum | solution.py:93
  281.3 30.5 %all_gather.23 = bf16[32,3,128]{0,2,1:T(8,128)(2,1)S(1)} all-gather(bf16[32,3,16]{0,2,1:T(8,128)(2,1)S(1)} %fusion.71), channel_id=1, replica_groups=mesh['row'=4,'col'=8] {'col'}, dimensions={2}, use_global_device_ids=true | all-gather | bytes 27648 | tf_op jit(solution)/shard_map/all_gather | solution.py:98
  311.9 5.5 %all_gather.22 = bf16[32,3,64]{0,2,1:T(8,128)(2,1)S(1)} all-gather(bf16[32,3,16]{0,2,1:T(8,128)(2,1)S(1)} %fusion.71), channel_id=1, replica_groups=mesh['row'=4,'col'=8] {'row'}, dimensions={2}, use_global_device_ids=true | all-gather | bytes 15360 | tf_op jit(solution)/shard_map/all_gather | solution.py:97
  317.6 0.7 while.31
  318.4 0.7 copy.46
  319.2 0.8 copy.45
  320.0 18.4 %reduce-scatter.11.cloned.1.call-done = f32[32,3,16]{0,2,1:T(8,128)} async-done(((f32[32,3,64]{0,2,1:T(8,128)}), f32[32,3,16]{0,2,1:T(8,128)}) %reduce-scatter.11.cloned.1.call-update) | async-done | bytes 6160 | tf_op jit(solution)/shard_map/reduce_scatter | solution.py:73
  338.4 65.2 %reduce-scatter.9.cloned.1.call-done = f32[32,3,16]{0,2,1:T(8,128)} async-done(((f32[32,3,128]{0,2,1:T(8,128)}), f32[32,3,16]{0,2,1:T(8,128)}) %reduce-scatter.9.cloned.1.call-update) | async-done | bytes 6160 | tf_op jit(solution)/shard_map/reduce_scatter | solution.py:72
  403.6 0.8 multiply_reduce_fusion
  404.4 40.2 %psum.31 = f32[32]{0:T(128)S(1)} all-reduce(f32[32]{0:T(128)S(1)} %multiply_reduce_fusion), channel_id=1, replica_groups=mesh['row'=4,'col'=8] {'row','col'}, use_global_device_ids=true, to_apply=%region_15.16 | all-reduce | flops 32 | bytes 256 | tf_op jit(solution)/shard_map/psum | solution.py:100
  444.6 0.6 add_multiply_fusion
  (57 shorter events, 2.1 us)
Async XLA Ops:
  6.5 129.4 %reduce-scatter.7.cloned.1.call-start = ((), (), s32[]{:S(2)}) async-start(), calls=%async_computation.5 | async-start | bytes 122880 | tf_op jit(solution)/shard_map/reduce_scatter | solution.py:73
  6.5 0.7 copy-start.3
  7.2 33.2 %copy-start = (f32[32,3,16]{0,2,1:T(8,128)S(1)}, f32[32,3,16]{0,2,1:T(8,128)}, u32[]{:S(2)}) copy-start(f32[32,3,16]{0,2,1:T(8,128)} %param.7) | copy-start | bytes 18436
  117.4 83.8 %reduce-scatter.5.cloned.1.call-start = ((), (), s32[]{:S(2)}) async-start(), calls=%async_computation.4 | async-start | bytes 221184 | tf_op jit(solution)/shard_map/reduce_scatter | solution.py:72
  118.3 220.2 %reduce-scatter.11.cloned.1.call-start = ((), (), s32[]{:S(2)}) async-start(), calls=%async_computation.7 | async-start | bytes 122880 | tf_op jit(solution)/shard_map/reduce_scatter | solution.py:73
  135.9 106.2 %copy-start.1 = (f32[32,3,16]{0,2,1:T(8,128)S(1)}, f32[32,3,16]{0,2,1:T(8,128)}, u32[]{:S(2)}) copy-start(f32[32,3,16]{0,2,1:T(8,128)} %reduce-scatter.7.cloned.1.call-done) | copy-start | bytes 18436
  201.2 40.9 %copy-start.2 = (f32[32,3,16]{0,2,1:T(8,128)S(1)}, f32[32,3,16]{0,2,1:T(8,128)}, u32[]{:S(2)}) copy-start(f32[32,3,16]{0,2,1:T(8,128)} %reduce-scatter.5.cloned.1.call-done) | copy-start | bytes 18436
  319.1 84.5 %reduce-scatter.9.cloned.1.call-start = ((), (), s32[]{:S(2)}) async-start(), calls=%async_computation.6 | async-start | bytes 221184 | tf_op jit(solution)/shard_map/reduce_scatter | solution.py:72
Sparse Core Ops, SparseCore 0:
  117.5 18.3 reduce-scatter.6
  139.2 61.9 reduce-scatter.4
  319.2 19.1 reduce-scatter.10
  341.6 61.9 reduce-scatter.8
where the time goes:
time: 453 us; the launch traced here: 452 us
  blocking collectives  264 us (58%)
  waiting for transfers between devices  167 us (37%)
  between operations  13.2 us (3%)
    reduce_scatter x2, waiting for transfers between devices, half_image(): lax.psum_scatter(sum_rows, 'col', scatter_dimension=2, tiled=True)  130 us
    psum x1, blocking collectives, on_device(): lax.psum(jnp.sum(basis_two * image_two, axis=(1, 2)), ('row', 'col'))  40.2 us
    psum x1, blocking collectives, on_device(): lax.psum(jnp.sum(basis_one * image_one, axis=(1, 2)), ('row', 'col'))  40.1 us
    psum x1, blocking collectives, on_device(): lax.psum(jnp.sum(remainder * remainder, axis=(1, 2)), ('row', 'col'))  39.1 us
    psum x1, blocking collectives, on_device(): lax.psum(jnp.sum(thermal_noise * thermal_noise, axis=(1, 2)), ('row', 'co...  38.9 us
    reduce_scatter x2, waiting for transfers between devices, half_image(): lax.psum_scatter(sum_cols, 'row', scatter_dimension=2, tiled=True)  36 us
    all_gather x1, blocking collectives, on_device(): lax.all_gather(basis_one, 'col', axis=2, tiled=True)  30.6 us
    all_gather x1, blocking collectives, on_device(): rows_two = lax.all_gather(narrow_two, 'col', axis=2, tiled=True)  30.5 us
  transfers between devices with their start and end apart: 4, of which 4 were waited for; matrix products, arithmetic and copies ran while one was open for 0% of the time, Pallas kernels for 0%

commit v1 on v0

--- a/solution.py
+++ b/solution.py
@@ -1,7 +1,16 @@
+import functools
 import jax
 import jax.numpy as jnp
 from jax import lax
 from jax.sharding import PartitionSpec as P
+
+
+def touch_the_zones(array_here, which_dim):
+    plain = lax.all_gather(array_here, axis_name="col")
+    return jnp.concatenate(plain, which_dim)
+
+
+part_run = functools.partial(touch_the_zones, which_dim=2)
 
 
 def pair_tensor(rows_pos, cols_pos, retain):
@@ -83,7 +92,7 @@
     )
     pos_rows, rows_wide = (
         lax.all_gather(positions, "col", axis=1, tiled=True),
-        lax.all_gather(basis_one, "col", axis=2, tiled=True),
+        part_run(basis_one),
     )
     image_one = half_image(
         pos_rows, pos_cols, rows_wide.astype(jnp.bfloat16), cols_one.astype(jnp.bfloat16), basis_one

time: 453 us -> 371 us (0.82)
  waiting for transfers between devices: 167 us -> 0 us
  blocking collectives: 264 us -> 360 us
  between operations: 13.2 us -> 1.5 us
    reduce_scatter x4 -> x0, waiting for transfers between devices: 166 us -> none  [the longest x2 130 us: half_image(): lax.psum_scatter(sum_rows, 'col', scatter_dimension=2, tiled=True)]
    unnamed x0 -> x4, blocking collectives: none -> 99.9 us
  transfers between devices with their start and end apart: 4 -> 0, of which waited for: 4 -> 0; matrix products, arithmetic and copies ran while one was open for 0% -> 0% of each run, Pallas kernels for 0% -> 0%
where the time goes in v1:
time: 371 us; the launch traced here: 369 us
  blocking collectives  360 us (97%)
  local copies, waits for them, and re-layouts  4.69 us (1%)
    unnamed x4, blocking collectives  99.9 us
    psum x1, blocking collectives, on_device(): lax.psum(jnp.sum(thermal_noise * thermal_noise, axis=(1, 2)), ('row', 'co...  42 us
    psum x1, blocking collectives, on_device(): lax.psum(jnp.sum(remainder * remainder, axis=(1, 2)), ('row', 'col'))  41 us
    psum x1, blocking collectives, on_device(): lax.psum(jnp.sum(basis_two * image_two, axis=(1, 2)), ('row', 'col'))  37 us
    psum x1, blocking collectives, on_device(): lax.psum(jnp.sum(basis_one * image_one, axis=(1, 2)), ('row', 'col'))  36.8 us
    all_gather x1, blocking collectives, touch_the_zones(): plain = lax.all_gather(array_here, axis_name='col')  30.8 us
    all_gather x1, blocking collectives, on_device(): rows_two = lax.all_gather(narrow_two, 'col', axis=2, tiled=True)  30.6 us
    all_gather x1, blocking collectives, on_device(): lax.all_gather(positions, 'col', axis=1, tiled=True)  26.1 us

profile of v1, /device:TPU:0, one launch (start us, length us, event | category | flops | bytes accessed | tf_op | source)
XLA Modules:
  0.0 368.9 jit_solution(11774549185331810694)
XLA Ops:
  0.0 0.7 copy-done
  0.8 42.0 %psum.28 = f32[32]{0:T(128)S(1)} all-reduce(f32[32]{0:T(128)S(1)} %multiply_reduce_fusion.2), channel_id=1, replica_groups=mesh['row'=4,'col'=8] {'row','col'}, use_global_device_ids=true, to_apply=%region_1.0 | all-reduce | flops 32 | bytes 256 | tf_op jit(solution)/shard_map/psum | solution.py:86
  42.9 30.8 %all-gather = bf16[256,3,16]{2,1,0:T(4,128)(2,1)S(1)} all-gather(bf16[32,3,16]{2,1,0:T(4,128)(2,1)S(1)} %copy.57), channel_id=2, replica_groups=mesh['row'=4,'col'=8] {'col'}, dimensions={0}, use_global_device_ids=true | all-gather | bytes 27648 | tf_op jit(solution)/shard_map/all_gather | solution.py:9
  74.0 5.5 %all_gather.23 = bf16[32,3,64]{0,2,1:T(8,128)(2,1)S(1)} all-gather(bf16[32,3,16]{0,2,1:T(8,128)(2,1)S(1)} %get-tuple-element.435), channel_id=1, replica_groups=mesh['row'=4,'col'=8] {'row'}, dimensions={2}, use_global_device_ids=true | all-gather | bytes 15360 | tf_op jit(solution)/shard_map/all_gather | solution.py:91
  79.6 0.6 copy-done.1
  80.2 26.1 %all-gather.1 = f32[8,16,3]{1,2,0:T(4,128)S(1)} all-gather(f32[1,16,3]{1,2,0:T(4,128)S(1)} %bitcast.141), channel_id=1, replica_groups=mesh['row'=4,'col'=8] {'col'}, dimensions={0}, use_global_device_ids=true | all-gather | bytes 1728 | tf_op jit(solution)/shard_map/all_gather | solution.py:94
  106.4 5.2 %all-gather.2 = f32[4,16,3]{1,2,0:T(4,128)S(1)} all-gather(f32[1,16,3]{1,2,0:T(4,128)S(1)} %bitcast.142), channel_id=1, replica_groups=mesh['row'=4,'col'=8] {'row'}, dimensions={0}, use_global_device_ids=true | all-gather | bytes 960 | tf_op jit(solution)/shard_map/all_gather | solution.py:90
  111.7 0.7 while.30
  112.2 0.2 fusion.91
  112.6 38.0 %all-reduce = f32[32,3,128]{0,1,2:T(4,128)S(1)} all-reduce(f32[32,3,128]{0,1,2:T(4,128)S(1)} %copy.61), channel_id=3, replica_groups=mesh['row'=4,'col'=8] {'col'}, use_global_device_ids=true, to_apply=%region_4.5.clone | all-reduce | flops 12288 | bytes 98304
  150.6 0.6 copy-done.3
  151.3 0.6 dynamic-slice
  152.7 11.7 %all-reduce.1 = f32[32,3,64]{0,1,2:T(4,128)S(1)} all-reduce(f32[32,3,64]{0,1,2:T(4,128)S(1)} %copy.63), channel_id=4, replica_groups=mesh['row'=4,'col'=8] {'row'}, use_global_device_ids=true, to_apply=%region_5.6.clone | all-reduce | flops 6144 | bytes 49152
  164.4 0.7 dynamic-slice.2
  165.8 36.8 %psum.29 = f32[32]{0:T(128)S(1)} all-reduce(f32[32]{0:T(128)S(1)} %get-tuple-element.433), channel_id=1, replica_groups=mesh['row'=4,'col'=8] {'row','col'}, use_global_device_ids=true, to_apply=%region_7.8 | all-reduce | flops 32 | bytes 256 | tf_op jit(solution)/shard_map/psum | solution.py:100
  202.6 41.0 %psum.30 = f32[32]{0:T(128)S(1)} all-reduce(f32[32]{0:T(128)S(1)} %multiply_reduce_fusion), channel_id=1, replica_groups=mesh['row'=4,'col'=8] {'row','col'}, use_global_device_ids=true, to_apply=%region_9.10 | all-reduce | flops 32 | bytes 256 | tf_op jit(solution)/shard_map/psum | solution.py:102
  243.6 30.6 %all_gather.27 = bf16[32,3,128]{0,2,1:T(8,128)(2,1)S(1)} all-gather(bf16[32,3,16]{0,2,1:T(8,128)(2,1)S(1)} %fusion.73), channel_id=1, replica_groups=mesh['row'=4,'col'=8] {'col'}, dimensions={2}, use_global_device_ids=true | all-gather | bytes 27648 | tf_op jit(solution)/shard_map/all_gather | solution.py:107
  274.3 5.5 %all_gather.26 = bf16[32,3,64]{0,2,1:T(8,128)(2,1)S(1)} all-gather(bf16[32,3,16]{0,2,1:T(8,128)(2,1)S(1)} %fusion.73), channel_id=1, replica_groups=mesh['row'=4,'col'=8] {'row'}, dimensions={2}, use_global_device_ids=true | all-gather | bytes 15360 | tf_op jit(solution)/shard_map/all_gather | solution.py:106
  279.9 0.7 while.31
  280.5 0.2 fusion.97
  280.8 38.7 %all-reduce.2 = f32[32,3,128]{0,1,2:T(4,128)S(1)} all-reduce(f32[32,3,128]{0,1,2:T(4,128)S(1)} %copy.67), channel_id=5, replica_groups=mesh['row'=4,'col'=8] {'col'}, use_global_device_ids=true, to_apply=%region_12.13.clone | all-reduce | flops 12288 | bytes 98304
  319.6 11.5 %all-reduce.3 = f32[32,3,64]{0,1,2:T(4,128)S(1)} all-reduce(f32[32,3,64]{0,1,2:T(4,128)S(1)} %copy.69), channel_id=6, replica_groups=mesh['row'=4,'col'=8] {'row'}, use_global_device_ids=true, to_apply=%region_13.14.clone | all-reduce | flops 6144 | bytes 49152
  331.2 37.0 %psum.31 = f32[32]{0:T(128)S(1)} all-reduce(f32[32]{0:T(128)S(1)} %fusion.71), channel_id=1, replica_groups=mesh['row'=4,'col'=8] {'row','col'}, use_global_device_ids=true, to_apply=%region_15.16 | all-reduce | flops 32 | bytes 256 | tf_op jit(solution)/shard_map/psum | solution.py:109
  368.2 0.6 add_multiply_fusion
  (56 shorter events, 2.4 us)
Async XLA Ops:
  0.0 0.7 copy-start
  79.5 0.7 copy-start.1
  150.6 0.7 copy-start.3
  152.7 11.7 %copy-start.2 = (u32[32]{0:T(128)S(1)}, u32[32]{0:T(128)}, u32[]{:S(2)}) copy-start(u32[32]{0:T(128)} %constant.271) | copy-start | bytes 388
